TPU v7x, 512 devices: a whole 4x4x16 slice. The times are simulated.
512 devices in a mesh: fine: 128 (over y, z, core), tele: 4 (over x).
Axes of the slice: x: 4, y: 4, z: 16, core: 2. Of those that a mesh axis runs over, the one named last changes fastest.
Arguments:
- right_side: float32 [8192, 320], P(('fine', 'tele')), may hold values from -6 to 6
- fine_inverse: bfloat16 [8192, 320, 320], P(('fine', 'tele')), may hold values from -0.08 to 0.45
- fine_links: int32 [8192, 6], P(('fine', 'tele')), may hold values from -1 to 8191, as said below
- fine_faces: int32 [8192, 6], P(('fine', 'tele')), may hold values from 0 to 23
- coarse_inverse: bfloat16 [1024, 320, 320], P(('fine', 'tele')), may hold values from -0.04 to 0.21
- coarse_links: int32 [1024, 6], P(('fine', 'tele')), may hold values from -1 to 1023, as said below
- coarse_faces: int32 [1024, 6], P(('fine', 'tele')), may hold values from 0 to 23
- face_operators: bfloat16 [24, 80, 80], replicated, may hold values from -1.25 to 1.25
- agglomerate: int32 [8192], P(('fine', 'tele')), may hold values from 0 to 1023, as said below
Outputs:
- solution: float32 [8192, 320], P(('fine', 'tele'))
Inputs may be any that keep to these rules, and one draw needn't show every extreme that they name: `fine_links`: any entry other than -1 is an element held by the same device as the element, or by the device just before or after it in the order of fine+tele, cyclically. `coarse_links`: coarse elements form blocks of 8 consecutive ones; any entry other than -1 lies in the element's own block or in the block just before or after it, cyclically. `agglomerate`: fine element i maps into block i // 64 of 8 consecutive coarse elements; every coarse element collects exactly 8 fine elements.
All inputs are finite; a program needn't handle non-finite values.
Results may differ from a plain program's by a relative error of at most 0.02.
Values may be sent and summed in bfloat16 or wider, within the bound.
No kernel may reach another device: no remote copies, remote signals or barrier semaphores. Data moves between devices by JAX's collectives and lax.ppermute only.
A program may use at most 64 MiB of HBM per device.

v0:
```python
import jax
import jax.numpy as jnp
from jax import lax
from jax.sharding import PartitionSpec as P

FIELDS = 5
NODES = 4
SWEEPS = 3
CYCLES = 2
OPPOSITE = (1, 0, 3, 2, 5, 4)


def passed_along(block, axis, distance):
    devices = range(lax.axis_size(axis))
    route = [((i - distance) % len(devices), i) for i in devices]
    return lax.ppermute(block, axis, route)


def face_table():
    face_size = NODES * NODES
    column = jnp.arange(6 * FIELDS * face_size, dtype=jnp.int32)
    face_index = column // (FIELDS * face_size)
    within = column % (FIELDS * face_size)
    field_index = within // face_size
    first = within // NODES % NODES
    second = within % NODES
    far_node = NODES - 1
    side = jnp.where(face_index % 2 == 0, 0, far_node)
    node_a = jnp.where(face_index < 2, side, first)
    node_b = jnp.where(face_index < 2, first, jnp.where(face_index < 4, side, second))
    node_c = jnp.where(face_index < 4, second, side)
    target = ((field_index * NODES + node_a) * NODES + node_b) * NODES + node_c
    dof_index = jnp.arange(FIELDS * NODES * NODES * NODES, dtype=jnp.int32)
    return (dof_index[:, None] == target[None, :]).astype(jnp.float32)


def take_traces(field_state, table):
    row_count = field_state.shape[0]
    picked = jnp.dot(
        field_state, table, precision=lax.Precision.HIGHEST, preferred_element_type=jnp.float32
    )
    return picked.astype(jnp.bfloat16).reshape(row_count, 6, -1)


def lift_faces(coupled, table):
    return lax.dot_general(
        coupled,
        table,
        (((1,), (1,)), ((), ())),
        precision=lax.Precision.HIGHEST,
        preferred_element_type=jnp.float32,
    )


def neighbour_rows(preceding, own_traces, following, links, position, row_count, devices):
    trace_pool = jnp.concatenate([preceding, own_traces, following], axis=0).reshape(
        -1, own_traces.shape[2]
    )
    clamped = jnp.maximum(links, 0)
    relative = (clamped // row_count - position + 1) % devices
    opposite = jnp.array(OPPOSITE, jnp.int32)
    row_index = (relative * row_count + clamped % row_count) * 6 + opposite[None, :]
    face_rows = jnp.take(trace_pool, row_index.reshape(-1), axis=0).reshape(links.shape[0], 6, -1)
    return jnp.where((links >= 0)[:, :, None], face_rows, jnp.zeros_like(face_rows))


def face_apply(face_operators, face_rows, faces, table):
    flat_rows = face_rows.reshape(-1, face_rows.shape[2])
    face_kinds = faces.reshape(-1)
    products = jnp.einsum(
        "rk,qjk->rqj", flat_rows, face_operators, preferred_element_type=jnp.float32
    )
    picked = face_kinds[:, None] == jnp.arange(face_operators.shape[0], dtype=jnp.int32)[None, :]
    result = jnp.sum(jnp.where(picked[:, :, None], products, 0.0), axis=1)
    return lift_faces(result.reshape(face_rows.shape[0], -1), table)


def fine_coupling(field_state, face_operators, links, faces, position, devices, table):
    own_traces = take_traces(field_state, table)
    preceding = passed_along(own_traces, ("fine", "tele"), 1)
    following = passed_along(own_traces, ("fine", "tele"), -1)
    face_rows = neighbour_rows(
        preceding, own_traces, following, links, position, field_state.shape[0], devices
    )
    return face_apply(face_operators, face_rows, faces, table)


def coarse_coupling(column_traces, face_operators, links, faces, position, devices, table):
    preceding = passed_along(column_traces, "fine", 1)
    following = passed_along(column_traces, "fine", -1)
    face_rows = neighbour_rows(
        preceding, column_traces, following, links, position, column_traces.shape[0], devices
    )
    return face_apply(face_operators, face_rows, faces, table)


def apply_inverse(inverse, lowered):
    return jnp.einsum("nij,nj->ni", inverse, lowered, preferred_element_type=jnp.float32)


def shards(
    right_side,
    fine_inverse,
    fine_links,
    fine_faces,
    coarse_inverse,
    coarse_links,
    coarse_faces,
    face_operators,
    agglomerate,
):
    table = face_table()
    tele_size = lax.axis_size("tele")
    fine_position = lax.axis_index("fine") * tele_size + lax.axis_index("tele")
    fine_devices = lax.axis_size("fine") * tele_size
    column_position = lax.axis_index("fine")
    columns = lax.axis_size("fine")
    column_rows = coarse_inverse.shape[0] * tele_size
    local_target = agglomerate % column_rows
    member = (local_target[:, None] == jnp.arange(column_rows, dtype=jnp.int32)[None, :]).astype(
        jnp.float32
    )
    block_inverse = lax.all_gather(coarse_inverse, "tele", axis=0, tiled=True)
    index_lists = lax.all_gather(
        jnp.concatenate([coarse_links, coarse_faces], axis=1), "tele", axis=0, tiled=True
    )
    block_links = index_lists[:, :6]
    block_faces = index_lists[:, 6:]
    solution = jnp.zeros(right_side.shape, jnp.float32)
    for cycle_index in range(CYCLES):
        for sweep_index in range(SWEEPS):
            if cycle_index == 0 and sweep_index == 0:
                coupled = jnp.zeros(right_side.shape, jnp.float32)
            else:
                coupled = fine_coupling(
                    solution,
                    face_operators,
                    fine_links,
                    fine_faces,
                    fine_position,
                    fine_devices,
                    table,
                )
            lowered = (right_side - coupled).astype(jnp.bfloat16)
            solution = apply_inverse(fine_inverse, lowered)
        residual = lowered.astype(jnp.float32) - fine_coupling(
            solution, face_operators, fine_links, fine_faces, fine_position, fine_devices, table
        )
        partial_sum = jnp.dot(
            member.T, residual, precision=lax.Precision.HIGHEST, preferred_element_type=jnp.float32
        )
        restricted = lax.psum(partial_sum, "tele")
        coarse_state = apply_inverse(block_inverse, restricted.astype(jnp.bfloat16))
        for sweep_index in range(SWEEPS - 1):
            coupled_coarse = coarse_coupling(
                take_traces(coarse_state, table),
                face_operators,
                block_links,
                block_faces,
                column_position,
                columns,
                table,
            )
            coarse_state = apply_inverse(
                block_inverse, (restricted - coupled_coarse).astype(jnp.bfloat16)
            )
        solution = solution + jnp.take(coarse_state, local_target, axis=0)
    return solution


def solution(mesh):
    return jax.shard_map(
        shards,
        mesh=mesh,
        in_specs=(
            P(("fine", "tele"), None),
            P(("fine", "tele"), None, None),
            P(("fine", "tele"), None),
            P(("fine", "tele"), None),
            P(("fine", "tele"), None, None),
            P(("fine", "tele"), None),
            P(("fine", "tele"), None),
            P(),
            P(("fine", "tele")),
        ),
        out_specs=P(("fine", "tele"), None),
        check_vma=False,
    )
```

profile of v0, /device:TPU:2, one launch (start us, length us, event | category | flops | bytes accessed | tf_op | source)
XLA Modules:
  0.0 242.5 jit_solution(18185007734287332940)
XLA Ops:
  7.5 3.3 %fusion.76 = f32[16,1,320]{2,1,0:T(1,128)S(1)} fusion(bf16[16,320,320]{2,1,0:T(8,128)(2,1)} %param.27, bf16[16,320,1]{1,0,2:T(8,128)(2,1)S(1)} %convert_bitcast_fusion), kind=kOutput, calls=%fused_computation.136 | convolution fusion | flops 3276800 | bytes 3307520 | tf_op jit(solution)/shard_map/nij,nj->ni/dot_general | solution.py:98
  11.3 7.8 %collective-permute-start.1 = (bf16[16,6,80]{2,1,0:T(8,128)(2,1)S(1)}, bf16[16,6,80]{2,1,0:T(8,128)(2,1)S(1)}, u32[]{:S(2)}, u32[]{:S(2)}) collective-permute-start(bf16[16,6,80]{2,1,0:T(8,128)(2,1)S(1)} %reshape.333), channel_id=1, source_target_pairs={{1,0},{2,1},{3,2},{4,3},{5,4},{6,5},{7,6},{8,7},{9,8},{10,9},{11,1... | collective-permute-start | bytes 46088 | tf_op jit(solution)/shard_map/ppermute | solution.py:16
  21.2 15.2 %all-gather = s32[4,2,12]{2,1,0:T(2,128)S(1)} all-gather(s32[1,2,12]{2,1,0:T(2,128)S(1)} %add_bitcast_fusion), channel_id=1, replica_groups=mesh['fine'=128,'tele'=4] {'tele'}, dimensions={0}, use_global_device_ids=true | all-gather | bytes 480 | tf_op jit(solution)/shard_map/all_gather | solution.py:124
  39.0 3.5 %fusion.73 = f32[16,1,320]{2,1,0:T(1,128)S(1)} fusion(bf16[16,320,320]{2,1,0:T(8,128)(2,1)} %param.27, bf16[16,320,1]{1,0,2:T(8,128)(2,1)S(1)} %fusion.18), kind=kOutput, calls=%fused_computation.133 | convolution fusion | flops 3276800 | bytes 3307520 | tf_op jit(solution)/shard_map/nij,nj->ni/dot_general | solution.py:98
  43.0 2.6 %collective-permute-start.3 = (bf16[16,6,80]{2,1,0:T(8,128)(2,1)S(1)}, bf16[16,6,80]{2,1,0:T(8,128)(2,1)S(1)}, u32[]{:S(2)}, u32[]{:S(2)}) collective-permute-start(bf16[16,6,80]{2,1,0:T(8,128)(2,1)S(1)} %reshape.337), channel_id=1, source_target_pairs={{1,0},{2,1},{3,2},{4,3},{5,4},{6,5},{7,6},{8,7},{9,8},{10,9},{11,1... | collective-permute-start | bytes 46088 | tf_op jit(solution)/shard_map/ppermute | solution.py:16
  45.5 3.3 %collective-permute-start.2 = (bf16[16,6,80]{2,1,0:T(8,128)(2,1)S(1)}, bf16[16,6,80]{2,1,0:T(8,128)(2,1)S(1)}, u32[]{:S(2)}, u32[]{:S(2)}) collective-permute-start(bf16[16,6,80]{2,1,0:T(8,128)(2,1)S(1)} %reshape.337), channel_id=1, source_target_pairs={{511,0},{0,1},{1,2},{2,3},{3,4},{4,5},{5,6},{6,7},{7,8},{8,9},{9,1... | collective-permute-start | bytes 46088 | tf_op jit(solution)/shard_map/ppermute | solution.py:16
  49.5 4.9 %collective-permute-done.2 = bf16[16,6,80]{2,1,0:T(8,128)(2,1)S(1)} collective-permute-done((bf16[16,6,80]{2,1,0:T(8,128)(2,1)S(1)}, bf16[16,6,80]{2,1,0:T(8,128)(2,1)S(1)}, u32[]{:S(2)}, u32[]{:S(2)}) %collective-permute-start.2) | collective-permute-done | bytes 15392 | tf_op jit(solution)/shard_map/ppermute | solution.py:16
  56.0 3.3 %fusion.70 = f32[16,1,320]{2,1,0:T(1,128)S(1)} fusion(bf16[16,320,320]{2,1,0:T(8,128)(2,1)} %param.27, bf16[16,320,1]{1,0,2:T(8,128)(2,1)S(1)} %bitcast.138), kind=kOutput, calls=%fused_computation.130 | convolution fusion | flops 3276800 | bytes 3307520 | tf_op jit(solution)/shard_map/nij,nj->ni/dot_general | solution.py:98
  59.8 8.2 %collective-permute-start.5 = (bf16[16,6,80]{2,1,0:T(8,128)(2,1)S(1)}, bf16[16,6,80]{2,1,0:T(8,128)(2,1)S(1)}, u32[]{:S(2)}, u32[]{:S(2)}) collective-permute-start(bf16[16,6,80]{2,1,0:T(8,128)(2,1)S(1)} %reshape.341), channel_id=1, source_target_pairs={{1,0},{2,1},{3,2},{4,3},{5,4},{6,5},{7,6},{8,7},{9,8},{10,9},{11,1... | collective-permute-start | bytes 46088 | tf_op jit(solution)/shard_map/ppermute | solution.py:16
  70.0 3.9 %collective-permute-done.4 = bf16[16,6,80]{2,1,0:T(8,128)(2,1)S(1)} collective-permute-done((bf16[16,6,80]{2,1,0:T(8,128)(2,1)S(1)}, bf16[16,6,80]{2,1,0:T(8,128)(2,1)S(1)}, u32[]{:S(2)}, u32[]{:S(2)}) %collective-permute-start.4) | collective-permute-done | bytes 15392 | tf_op jit(solution)/shard_map/ppermute | solution.py:16
  75.8 17.8 %psum.14 = f32[8,320]{1,0:T(8,128)S(1)} all-reduce(f32[8,320]{1,0:T(8,128)S(1)} %fusion.145), channel_id=1, replica_groups=mesh['fine'=128,'tele'=4] {'tele'}, use_global_device_ids=true, to_apply=%region_3.5 | all-reduce | flops 2560 | bytes 20480 | tf_op jit(solution)/shard_map/psum | solution.py:152
  98.2 2.4 collective-permute-start.6
  100.8 5.9 %collective-permute-done.6 = bf16[8,6,80]{2,1,0:T(8,128)(2,1)S(1)} collective-permute-done((bf16[8,6,80]{2,1,0:T(8,128)(2,1)S(1)}, bf16[8,6,80]{2,1,0:T(8,128)(2,1)S(1)}, u32[]{:S(2)}, u32[]{:S(2)}) %collective-permute-start.6) | collective-permute-done | bytes 7712 | tf_op jit(solution)/shard_map/ppermute | solution.py:16
  112.8 2.4 collective-permute-start.8
  115.3 5.9 %collective-permute-done.8 = bf16[8,6,80]{2,1,0:T(8,128)(2,1)S(1)} collective-permute-done((bf16[8,6,80]{2,1,0:T(8,128)(2,1)S(1)}, bf16[8,6,80]{2,1,0:T(8,128)(2,1)S(1)}, u32[]{:S(2)}, u32[]{:S(2)}) %collective-permute-start.8) | collective-permute-done | bytes 7712 | tf_op jit(solution)/shard_map/ppermute | solution.py:16
  124.5 3.3 %collective-permute-start.11 = (bf16[16,6,80]{2,1,0:T(8,128)(2,1)S(1)}, bf16[16,6,80]{2,1,0:T(8,128)(2,1)S(1)}, u32[]{:S(2)}, u32[]{:S(2)}) collective-permute-start(bf16[16,6,80]{2,1,0:T(8,128)(2,1)S(1)} %reshape.353), channel_id=1, source_target_pairs={{1,0},{2,1},{3,2},{4,3},{5,4},{6,5},{7,6},{8,7},{9,8},{10,9},{11,1... | collective-permute-start | bytes 46088 | tf_op jit(solution)/shard_map/ppermute | solution.py:16
  127.9 2.5 %collective-permute-start.10 = (bf16[16,6,80]{2,1,0:T(8,128)(2,1)S(1)}, bf16[16,6,80]{2,1,0:T(8,128)(2,1)S(1)}, u32[]{:S(2)}, u32[]{:S(2)}) collective-permute-start(bf16[16,6,80]{2,1,0:T(8,128)(2,1)S(1)} %reshape.353), channel_id=1, source_target_pairs={{511,0},{0,1},{1,2},{2,3},{3,4},{4,5},{5,6},{6,7},{7,8},{8,9},{9,1... | collective-permute-start | bytes 46088 | tf_op jit(solution)/shard_map/ppermute | solution.py:16
  130.4 3.3 %collective-permute-done.10 = bf16[16,6,80]{2,1,0:T(8,128)(2,1)S(1)} collective-permute-done((bf16[16,6,80]{2,1,0:T(8,128)(2,1)S(1)}, bf16[16,6,80]{2,1,0:T(8,128)(2,1)S(1)}, u32[]{:S(2)}, u32[]{:S(2)}) %collective-permute-start.10) | collective-permute-done | bytes 15392 | tf_op jit(solution)/shard_map/ppermute | solution.py:16
  135.4 3.3 %fusion.68 = f32[16,1,320]{2,1,0:T(1,128)S(1)} fusion(bf16[16,320,320]{2,1,0:T(8,128)(2,1)} %param.27, bf16[16,320,1]{1,0,2:T(8,128)(2,1)S(1)} %fusion.17), kind=kOutput, calls=%fused_computation.128 | convolution fusion | flops 3276800 | bytes 3307520 | tf_op jit(solution)/shard_map/nij,nj->ni/dot_general | solution.py:98
  139.1 6.9 %collective-permute-start.13 = (bf16[16,6,80]{2,1,0:T(8,128)(2,1)S(1)}, bf16[16,6,80]{2,1,0:T(8,128)(2,1)S(1)}, u32[]{:S(2)}, u32[]{:S(2)}) collective-permute-start(bf16[16,6,80]{2,1,0:T(8,128)(2,1)S(1)} %reshape.357), channel_id=1, source_target_pairs={{1,0},{2,1},{3,2},{4,3},{5,4},{6,5},{7,6},{8,7},{9,8},{10,9},{11,1... | collective-permute-start | bytes 46088 | tf_op jit(solution)/shard_map/ppermute | solution.py:16
  148.2 3.7 %collective-permute-done.12 = bf16[16,6,80]{2,1,0:T(8,128)(2,1)S(1)} collective-permute-done((bf16[16,6,80]{2,1,0:T(8,128)(2,1)S(1)}, bf16[16,6,80]{2,1,0:T(8,128)(2,1)S(1)}, u32[]{:S(2)}, u32[]{:S(2)}) %collective-permute-start.12) | collective-permute-done | bytes 15392 | tf_op jit(solution)/shard_map/ppermute | solution.py:16
  153.5 3.3 %fusion.65 = f32[16,1,320]{2,1,0:T(1,128)S(1)} fusion(bf16[16,320,320]{2,1,0:T(8,128)(2,1)} %param.27, bf16[16,320,1]{1,0,2:T(8,128)(2,1)S(1)} %fusion.16), kind=kOutput, calls=%fused_computation.125 | convolution fusion | flops 3276800 | bytes 3307520 | tf_op jit(solution)/shard_map/nij,nj->ni/dot_general | solution.py:98
  157.3 6.8 %collective-permute-start.15 = (bf16[16,6,80]{2,1,0:T(8,128)(2,1)S(1)}, bf16[16,6,80]{2,1,0:T(8,128)(2,1)S(1)}, u32[]{:S(2)}, u32[]{:S(2)}) collective-permute-start(bf16[16,6,80]{2,1,0:T(8,128)(2,1)S(1)} %reshape.361), channel_id=1, source_target_pairs={{1,0},{2,1},{3,2},{4,3},{5,4},{6,5},{7,6},{8,7},{9,8},{10,9},{11,1... | collective-permute-start | bytes 46088 | tf_op jit(solution)/shard_map/ppermute | solution.py:16
  166.0 3.9 %collective-permute-done.14 = bf16[16,6,80]{2,1,0:T(8,128)(2,1)S(1)} collective-permute-done((bf16[16,6,80]{2,1,0:T(8,128)(2,1)S(1)}, bf16[16,6,80]{2,1,0:T(8,128)(2,1)S(1)}, u32[]{:S(2)}, u32[]{:S(2)}) %collective-permute-start.14) | collective-permute-done | bytes 15392 | tf_op jit(solution)/shard_map/ppermute | solution.py:16
  171.6 3.3 %fusion.62 = f32[16,1,320]{2,1,0:T(1,128)S(1)} fusion(bf16[16,320,320]{2,1,0:T(8,128)(2,1)} %param.27, bf16[16,320,1]{1,0,2:T(8,128)(2,1)S(1)} %bitcast.137), kind=kOutput, calls=%fused_computation.122 | convolution fusion | flops 3276800 | bytes 3307520 | tf_op jit(solution)/shard_map/nij,nj->ni/dot_general | solution.py:98
  175.3 6.8 %collective-permute-start.17 = (bf16[16,6,80]{2,1,0:T(8,128)(2,1)S(1)}, bf16[16,6,80]{2,1,0:T(8,128)(2,1)S(1)}, u32[]{:S(2)}, u32[]{:S(2)}) collective-permute-start(bf16[16,6,80]{2,1,0:T(8,128)(2,1)S(1)} %reshape.365), channel_id=1, source_target_pairs={{1,0},{2,1},{3,2},{4,3},{5,4},{6,5},{7,6},{8,7},{9,8},{10,9},{11,1... | collective-permute-start | bytes 46088 | tf_op jit(solution)/shard_map/ppermute | solution.py:16
  184.1 3.9 %collective-permute-done.16 = bf16[16,6,80]{2,1,0:T(8,128)(2,1)S(1)} collective-permute-done((bf16[16,6,80]{2,1,0:T(8,128)(2,1)S(1)}, bf16[16,6,80]{2,1,0:T(8,128)(2,1)S(1)}, u32[]{:S(2)}, u32[]{:S(2)}) %collective-permute-start.16) | collective-permute-done | bytes 15392 | tf_op jit(solution)/shard_map/ppermute | solution.py:16
  190.0 17.7 %psum.15 = f32[8,320]{1,0:T(8,128)S(1)} all-reduce(f32[8,320]{1,0:T(8,128)S(1)} %fusion.144), channel_id=1, replica_groups=mesh['fine'=128,'tele'=4] {'tele'}, use_global_device_ids=true, to_apply=%region_10.14 | all-reduce | flops 2560 | bytes 20480 | tf_op jit(solution)/shard_map/psum | solution.py:152
  210.6 2.4 collective-permute-start.18
  213.1 6.0 %collective-permute-done.18 = bf16[8,6,80]{2,1,0:T(8,128)(2,1)S(1)} collective-permute-done((bf16[8,6,80]{2,1,0:T(8,128)(2,1)S(1)}, bf16[8,6,80]{2,1,0:T(8,128)(2,1)S(1)}, u32[]{:S(2)}, u32[]{:S(2)}) %collective-permute-start.18) | collective-permute-done | bytes 7712 | tf_op jit(solution)/shard_map/ppermute | solution.py:16
  223.7 2.4 collective-permute-start.20
  226.1 6.0 %collective-permute-done.20 = bf16[8,6,80]{2,1,0:T(8,128)(2,1)S(1)} collective-permute-done((bf16[8,6,80]{2,1,0:T(8,128)(2,1)S(1)}, bf16[8,6,80]{2,1,0:T(8,128)(2,1)S(1)}, u32[]{:S(2)}, u32[]{:S(2)}) %collective-permute-start.20) | collective-permute-done | bytes 7712 | tf_op jit(solution)/shard_map/ppermute | solution.py:16
  (179 shorter events, 52.6 us)
Async XLA Ops:
  6.5 31.5 %copy-start = (bf16[24,80,80]{2,1,0:T(8,128)(2,1)S(1)}, bf16[24,80,80]{2,1,0:T(8,128)(2,1)}, u32[]{:S(2)}) copy-start(bf16[24,80,80]{2,1,0:T(8,128)(2,1)} %param.33) | copy-start | bytes 921604
  6.5 29.8 %copy-start.5 = (s32[6]{0:T(128)S(1)}, s32[6]{0:T(128)}, u32[]{:S(2)}) copy-start(s32[6]{0:T(128)} %constant.277.clone) | copy-start | bytes 76
  6.5 32.1 %copy-start.2 = (f32[16,320]{1,0:T(8,128)S(1)}, f32[16,320]{1,0:T(8,128)}, u32[]{:S(2)}) copy-start(f32[16,320]{1,0:T(8,128)} %param.26) | copy-start | bytes 61444
  6.5 14.5 %copy-start.3 = (s32[16,6]{0,1:T(8,128)S(1)}, s32[16,6]{0,1:T(8,128)}, u32[]{:S(2)}) copy-start(s32[16,6]{0,1:T(8,128)} %param.28) | copy-start | bytes 1156
  6.5 14.5 %copy-start.6 = (s32[2,6]{1,0:T(2,128)S(1)}, s32[2,6]{1,0:T(2,128)}, u32[]{:S(2)}) copy-start(s32[2,6]{1,0:T(2,128)} %param.32) | copy-start | bytes 148
  6.5 14.5 %copy-start.7 = (s32[2,6]{1,0:T(2,128)S(1)}, s32[2,6]{1,0:T(2,128)}, u32[]{:S(2)}) copy-start(s32[2,6]{1,0:T(2,128)} %param.31) | copy-start | bytes 148
  6.6 30.1 %copy-start.8 = (s32[16]{0:T(128)S(1)}, s32[16]{0:T(128)}, u32[]{:S(2)}) copy-start(s32[16]{0:T(128)} %param.34) | copy-start | bytes 196
  6.6 30.3 %copy-start.4 = (s32[16,6]{0,1:T(8,128)S(1)}, s32[16,6]{0,1:T(8,128)}, u32[]{:S(2)}) copy-start(s32[16,6]{0,1:T(8,128)} %param.29) | copy-start | bytes 1156
  6.6 87.0 %all-gather.3.cloned.1.call-start = ((), (), s32[]{:S(2)}) async-start(), calls=%async_computation | async-start | bytes 2457600 | tf_op jit(solution)/shard_map/all_gather | solution.py:123
  11.3 26.0 %collective-permute-start.1 = (bf16[16,6,80]{2,1,0:T(8,128)(2,1)S(1)}, bf16[16,6,80]{2,1,0:T(8,128)(2,1)S(1)}, u32[]{:S(2)}, u32[]{:S(2)}) collective-permute-start(bf16[16,6,80]{2,1,0:T(8,128)(2,1)S(1)} %reshape.333), channel_id=1, source_target_pairs={{1,0},{2,1},{3,2},{4,3},{5,4},{6,5},{7,6},{8,7},{9,8},{10,9},{11,1... | collective-permute-start | bytes 46088 | tf_op jit(solution)/shard_map/ppermute | solution.py:16
  19.1 18.2 %collective-permute-start = (bf16[16,6,80]{2,1,0:T(8,128)(2,1)S(1)}, bf16[16,6,80]{2,1,0:T(8,128)(2,1)S(1)}, u32[]{:S(2)}, u32[]{:S(2)}) collective-permute-start(bf16[16,6,80]{2,1,0:T(8,128)(2,1)S(1)} %reshape.333), channel_id=1, source_target_pairs={{511,0},{0,1},{1,2},{2,3},{3,4},{4,5},{5,6},{6,7},{7,8},{8,9},{9,1... | collective-permute-start | bytes 46088 | tf_op jit(solution)/shard_map/ppermute | solution.py:16
  43.0 6.5 %collective-permute-start.3 = (bf16[16,6,80]{2,1,0:T(8,128)(2,1)S(1)}, bf16[16,6,80]{2,1,0:T(8,128)(2,1)S(1)}, u32[]{:S(2)}, u32[]{:S(2)}) collective-permute-start(bf16[16,6,80]{2,1,0:T(8,128)(2,1)S(1)} %reshape.337), channel_id=1, source_target_pairs={{1,0},{2,1},{3,2},{4,3},{5,4},{6,5},{7,6},{8,7},{9,8},{10,9},{11,1... | collective-permute-start | bytes 46088 | tf_op jit(solution)/shard_map/ppermute | solution.py:16
  45.5 8.8 %collective-permute-start.2 = (bf16[16,6,80]{2,1,0:T(8,128)(2,1)S(1)}, bf16[16,6,80]{2,1,0:T(8,128)(2,1)S(1)}, u32[]{:S(2)}, u32[]{:S(2)}) collective-permute-start(bf16[16,6,80]{2,1,0:T(8,128)(2,1)S(1)} %reshape.337), channel_id=1, source_target_pairs={{511,0},{0,1},{1,2},{2,3},{3,4},{4,5},{5,6},{6,7},{7,8},{8,9},{9,1... | collective-permute-start | bytes 46088 | tf_op jit(solution)/shard_map/ppermute | solution.py:16
  59.8 10.2 %collective-permute-start.5 = (bf16[16,6,80]{2,1,0:T(8,128)(2,1)S(1)}, bf16[16,6,80]{2,1,0:T(8,128)(2,1)S(1)}, u32[]{:S(2)}, u32[]{:S(2)}) collective-permute-start(bf16[16,6,80]{2,1,0:T(8,128)(2,1)S(1)} %reshape.341), channel_id=1, source_target_pairs={{1,0},{2,1},{3,2},{4,3},{5,4},{6,5},{7,6},{8,7},{9,8},{10,9},{11,1... | collective-permute-start | bytes 46088 | tf_op jit(solution)/shard_map/ppermute | solution.py:16
  68.0 5.8 %collective-permute-start.4 = (bf16[16,6,80]{2,1,0:T(8,128)(2,1)S(1)}, bf16[16,6,80]{2,1,0:T(8,128)(2,1)S(1)}, u32[]{:S(2)}, u32[]{:S(2)}) collective-permute-start(bf16[16,6,80]{2,1,0:T(8,128)(2,1)S(1)} %reshape.341), channel_id=1, source_target_pairs={{511,0},{0,1},{1,2},{2,3},{3,4},{4,5},{5,6},{6,7},{7,8},{8,9},{9,1... | collective-permute-start | bytes 46088 | tf_op jit(solution)/shard_map/ppermute | solution.py:16
  93.6 29.3 %copy-start.1 = (bf16[8,320,320]{2,1,0:T(8,128)(2,1)S(1)}, bf16[8,320,320]{2,1,0:T(8,128)(2,1)}, u32[]{:S(2)}) copy-start(bf16[8,320,320]{2,1,0:T(8,128)(2,1)} %all-gather.3.cloned.1.call-done) | copy-start | bytes 4915204
  96.3 4.4 %collective-permute-start.7 = (bf16[8,6,80]{2,1,0:T(8,128)(2,1)S(1)}, bf16[8,6,80]{2,1,0:T(8,128)(2,1)S(1)}, u32[]{:S(2)}, u32[]{:S(2)}) collective-permute-start(bf16[8,6,80]{2,1,0:T(8,128)(2,1)S(1)} %reshape.345), channel_id=1, source_target_pairs={{4,0},{8,4},{12,8},{16,12},{20,16},{24,20},{28,24},{32,28},{36,32}... | collective-permute-start | bytes 23048 | tf_op jit(solution)/shard_map/ppermute | solution.py:16
  98.2 8.4 %collective-permute-start.6 = (bf16[8,6,80]{2,1,0:T(8,128)(2,1)S(1)}, bf16[8,6,80]{2,1,0:T(8,128)(2,1)S(1)}, u32[]{:S(2)}, u32[]{:S(2)}) collective-permute-start(bf16[8,6,80]{2,1,0:T(8,128)(2,1)S(1)} %reshape.345), channel_id=1, source_target_pairs={{508,0},{0,4},{4,8},{8,12},{12,16},{16,20},{20,24},{24,28},{28,32}... | collective-permute-start | bytes 23048 | tf_op jit(solution)/shard_map/ppermute | solution.py:16
  110.9 4.4 %collective-permute-start.9 = (bf16[8,6,80]{2,1,0:T(8,128)(2,1)S(1)}, bf16[8,6,80]{2,1,0:T(8,128)(2,1)S(1)}, u32[]{:S(2)}, u32[]{:S(2)}) collective-permute-start(bf16[8,6,80]{2,1,0:T(8,128)(2,1)S(1)} %reshape.349), channel_id=1, source_target_pairs={{4,0},{8,4},{12,8},{16,12},{20,16},{24,20},{28,24},{32,28},{36,32}... | collective-permute-start | bytes 23048 | tf_op jit(solution)/shard_map/ppermute | solution.py:16
  112.8 8.4 %collective-permute-start.8 = (bf16[8,6,80]{2,1,0:T(8,128)(2,1)S(1)}, bf16[8,6,80]{2,1,0:T(8,128)(2,1)S(1)}, u32[]{:S(2)}, u32[]{:S(2)}) collective-permute-start(bf16[8,6,80]{2,1,0:T(8,128)(2,1)S(1)} %reshape.349), channel_id=1, source_target_pairs={{508,0},{0,4},{4,8},{8,12},{12,16},{16,20},{20,24},{24,28},{28,32}... | collective-permute-start | bytes 23048 | tf_op jit(solution)/shard_map/ppermute | solution.py:16
  124.5 5.9 %collective-permute-start.11 = (bf16[16,6,80]{2,1,0:T(8,128)(2,1)S(1)}, bf16[16,6,80]{2,1,0:T(8,128)(2,1)S(1)}, u32[]{:S(2)}, u32[]{:S(2)}) collective-permute-start(bf16[16,6,80]{2,1,0:T(8,128)(2,1)S(1)} %reshape.353), channel_id=1, source_target_pairs={{1,0},{2,1},{3,2},{4,3},{5,4},{6,5},{7,6},{8,7},{9,8},{10,9},{11,1... | collective-permute-start | bytes 46088 | tf_op jit(solution)/shard_map/ppermute | solution.py:16
  127.9 5.8 %collective-permute-start.10 = (bf16[16,6,80]{2,1,0:T(8,128)(2,1)S(1)}, bf16[16,6,80]{2,1,0:T(8,128)(2,1)S(1)}, u32[]{:S(2)}, u32[]{:S(2)}) collective-permute-start(bf16[16,6,80]{2,1,0:T(8,128)(2,1)S(1)} %reshape.353), channel_id=1, source_target_pairs={{511,0},{0,1},{1,2},{2,3},{3,4},{4,5},{5,6},{6,7},{7,8},{8,9},{9,1... | collective-permute-start | bytes 46088 | tf_op jit(solution)/shard_map/ppermute | solution.py:16
  139.1 9.0 %collective-permute-start.13 = (bf16[16,6,80]{2,1,0:T(8,128)(2,1)S(1)}, bf16[16,6,80]{2,1,0:T(8,128)(2,1)S(1)}, u32[]{:S(2)}, u32[]{:S(2)}) collective-permute-start(bf16[16,6,80]{2,1,0:T(8,128)(2,1)S(1)} %reshape.357), channel_id=1, source_target_pairs={{1,0},{2,1},{3,2},{4,3},{5,4},{6,5},{7,6},{8,7},{9,8},{10,9},{11,1... | collective-permute-start | bytes 46088 | tf_op jit(solution)/shard_map/ppermute | solution.py:16
  146.0 5.8 %collective-permute-start.12 = (bf16[16,6,80]{2,1,0:T(8,128)(2,1)S(1)}, bf16[16,6,80]{2,1,0:T(8,128)(2,1)S(1)}, u32[]{:S(2)}, u32[]{:S(2)}) collective-permute-start(bf16[16,6,80]{2,1,0:T(8,128)(2,1)S(1)} %reshape.357), channel_id=1, source_target_pairs={{511,0},{0,1},{1,2},{2,3},{3,4},{4,5},{5,6},{6,7},{7,8},{8,9},{9,1... | collective-permute-start | bytes 46088 | tf_op jit(solution)/shard_map/ppermute | solution.py:16
  157.3 8.7 %collective-permute-start.15 = (bf16[16,6,80]{2,1,0:T(8,128)(2,1)S(1)}, bf16[16,6,80]{2,1,0:T(8,128)(2,1)S(1)}, u32[]{:S(2)}, u32[]{:S(2)}) collective-permute-start(bf16[16,6,80]{2,1,0:T(8,128)(2,1)S(1)} %reshape.361), channel_id=1, source_target_pairs={{1,0},{2,1},{3,2},{4,3},{5,4},{6,5},{7,6},{8,7},{9,8},{10,9},{11,1... | collective-permute-start | bytes 46088 | tf_op jit(solution)/shard_map/ppermute | solution.py:16
  164.1 5.8 %collective-permute-start.14 = (bf16[16,6,80]{2,1,0:T(8,128)(2,1)S(1)}, bf16[16,6,80]{2,1,0:T(8,128)(2,1)S(1)}, u32[]{:S(2)}, u32[]{:S(2)}) collective-permute-start(bf16[16,6,80]{2,1,0:T(8,128)(2,1)S(1)} %reshape.361), channel_id=1, source_target_pairs={{511,0},{0,1},{1,2},{2,3},{3,4},{4,5},{5,6},{6,7},{7,8},{8,9},{9,1... | collective-permute-start | bytes 46088 | tf_op jit(solution)/shard_map/ppermute | solution.py:16
  175.3 8.7 %collective-permute-start.17 = (bf16[16,6,80]{2,1,0:T(8,128)(2,1)S(1)}, bf16[16,6,80]{2,1,0:T(8,128)(2,1)S(1)}, u32[]{:S(2)}, u32[]{:S(2)}) collective-permute-start(bf16[16,6,80]{2,1,0:T(8,128)(2,1)S(1)} %reshape.365), channel_id=1, source_target_pairs={{1,0},{2,1},{3,2},{4,3},{5,4},{6,5},{7,6},{8,7},{9,8},{10,9},{11,1... | collective-permute-start | bytes 46088 | tf_op jit(solution)/shard_map/ppermute | solution.py:16
  182.1 5.9 %collective-permute-start.16 = (bf16[16,6,80]{2,1,0:T(8,128)(2,1)S(1)}, bf16[16,6,80]{2,1,0:T(8,128)(2,1)S(1)}, u32[]{:S(2)}, u32[]{:S(2)}) collective-permute-start(bf16[16,6,80]{2,1,0:T(8,128)(2,1)S(1)} %reshape.365), channel_id=1, source_target_pairs={{511,0},{0,1},{1,2},{2,3},{3,4},{4,5},{5,6},{6,7},{7,8},{8,9},{9,1... | collective-permute-start | bytes 46088 | tf_op jit(solution)/shard_map/ppermute | solution.py:16
  208.7 4.3 %collective-permute-start.19 = (bf16[8,6,80]{2,1,0:T(8,128)(2,1)S(1)}, bf16[8,6,80]{2,1,0:T(8,128)(2,1)S(1)}, u32[]{:S(2)}, u32[]{:S(2)}) collective-permute-start(bf16[8,6,80]{2,1,0:T(8,128)(2,1)S(1)} %reshape.369), channel_id=1, source_target_pairs={{4,0},{8,4},{12,8},{16,12},{20,16},{24,20},{28,24},{32,28},{36,32}... | collective-permute-start | bytes 23048 | tf_op jit(solution)/shard_map/ppermute | solution.py:16
  210.6 8.4 %collective-permute-start.18 = (bf16[8,6,80]{2,1,0:T(8,128)(2,1)S(1)}, bf16[8,6,80]{2,1,0:T(8,128)(2,1)S(1)}, u32[]{:S(2)}, u32[]{:S(2)}) collective-permute-start(bf16[8,6,80]{2,1,0:T(8,128)(2,1)S(1)} %reshape.369), channel_id=1, source_target_pairs={{508,0},{0,4},{4,8},{8,12},{12,16},{16,20},{20,24},{24,28},{28,32}... | collective-permute-start | bytes 23048 | tf_op jit(solution)/shard_map/ppermute | solution.py:16
  221.8 4.3 %collective-permute-start.21 = (bf16[8,6,80]{2,1,0:T(8,128)(2,1)S(1)}, bf16[8,6,80]{2,1,0:T(8,128)(2,1)S(1)}, u32[]{:S(2)}, u32[]{:S(2)}) collective-permute-start(bf16[8,6,80]{2,1,0:T(8,128)(2,1)S(1)} %reshape.373), channel_id=1, source_target_pairs={{4,0},{8,4},{12,8},{16,12},{20,16},{24,20},{28,24},{32,28},{36,32}... | collective-permute-start | bytes 23048 | tf_op jit(solution)/shard_map/ppermute | solution.py:16
  223.7 8.4 %collective-permute-start.20 = (bf16[8,6,80]{2,1,0:T(8,128)(2,1)S(1)}, bf16[8,6,80]{2,1,0:T(8,128)(2,1)S(1)}, u32[]{:S(2)}, u32[]{:S(2)}) collective-permute-start(bf16[8,6,80]{2,1,0:T(8,128)(2,1)S(1)} %reshape.373), channel_id=1, source_target_pairs={{508,0},{0,4},{4,8},{8,12},{12,16},{16,20},{20,24},{24,28},{28,32}... | collective-permute-start | bytes 23048 | tf_op jit(solution)/shard_map/ppermute | solution.py:16
Sparse Core Ops, SparseCore 0:
  21.2 38.3 all-gather.2
where the time goes:
time: 244 us; the launch traced here: 243 us
  starting transfers between devices  75.3 us (31%)
  blocking collectives  50.6 us (21%)
  waiting for transfers between devices  47.8 us (20%)
  matrix products  40.2 us (16%)
  between operations  14.2 us (6%)
  local copies, waits for them, and re-layouts  12.1 us (5%)
    ppermute x22, starting transfers between devices, passed_along(): return lax.ppermute(block, axis, route)  75.3 us
    ppermute x22, waiting for transfers between devices, passed_along(): return lax.ppermute(block, axis, route)  47.8 us
    psum x2, blocking collectives, shards(): restricted = lax.psum(partial_sum, 'tele')  35.5 us
    dot_general x12, matrix products, apply_inverse(): jnp.einsum('nij,nj->ni', inverse, lowered, preferred_element_type=jnp.flo...  27.4 us
    all_gather x1, blocking collectives, shards(): lax.all_gather(jnp.concatenate([coarse_links, coarse_faces], axis=1), 'te...  15.2 us
    gather x11, local copies, waits for them, and re-layouts, neighbour_rows(): jnp.take(trace_pool, row_index.reshape(-1), axis=0)  7.19 us
  transfers between devices with their start and end apart: 23, of which 11 were waited for; matrix products, arithmetic and copies ran while one was open for 6% of the time, Pallas kernels for 0%

commit v1 on v0

--- a/solution.py
+++ b/solution.py
@@ -121,8 +121,16 @@
         jnp.float32
     )
     block_inverse = lax.all_gather(coarse_inverse, "tele", axis=0, tiled=True)
-    index_lists = lax.all_gather(
-        jnp.concatenate([coarse_links, coarse_faces], axis=1), "tele", axis=0, tiled=True
+    index_lists = jnp.concatenate(
+        lax.all_to_all(
+            jnp.stack(
+                [jnp.concatenate([coarse_links, coarse_faces], axis=1)] * lax.axis_size("tele")
+            ),
+            "tele",
+            0,
+            0,
+        ),
+        axis=0,
     )
     block_links = index_lists[:, :6]
     block_faces = index_lists[:, 6:]

time: 244 us -> 245 us (level)
  blocking collectives: 50.6 us -> 35.5 us
  starting transfers between devices: 75.3 us -> 86.7 us
  waiting for transfers between devices: 47.8 us -> 52.1 us
    all_gather x1 -> x0, blocking collectives: 15.2 us -> none  [shards(): lax.all_gather(jnp.concatenate([coarse_links, coarse_faces], axis=1), 'te...]
    all_to_all x0 -> x1, starting transfers between devices: none -> 11.4 us  [shards(): lax.all_to_all(jnp.stack([jnp.concatenate([coarse_links, coarse_faces], a...]
    all_to_all x0 -> x1, waiting for transfers between devices: none -> 3.11 us  [shards(): lax.all_to_all(jnp.stack([jnp.concatenate([coarse_links, coarse_faces], a...]
  transfers between devices with their start and end apart: 23 -> 24, of which waited for: 11 -> 12; matrix products, arithmetic and copies ran while one was open for 6% -> 6% of each run, Pallas kernels for 0% -> 0%
where the time goes in v1:
time: 245 us; the launch traced here: 244 us
  starting transfers between devices  86.7 us (35%)
  waiting for transfers between devices  52.1 us (21%)
  matrix products  40.2 us (16%)
  blocking collectives  35.5 us (14%)
  between operations  14.2 us (6%)
  local copies, waits for them, and re-layouts  12.7 us (5%)
    ppermute x22, starting transfers between devices, passed_along(): return lax.ppermute(block, axis, route)  75.3 us
    ppermute x22, waiting for transfers between devices, passed_along(): return lax.ppermute(block, axis, route)  49 us
    psum x2, blocking collectives, shards(): restricted = lax.psum(partial_sum, 'tele')  35.5 us
    dot_general x12, matrix products, apply_inverse(): jnp.einsum('nij,nj->ni', inverse, lowered, preferred_element_type=jnp.flo...  27.4 us
    all_to_all x1, starting transfers between devices, shards(): lax.all_to_all(jnp.stack([jnp.concatenate([coarse_links, coarse_faces], a...  11.4 us
    gather x11, local copies, waits for them, and re-layouts, neighbour_rows(): jnp.take(trace_pool, row_index.reshape(-1), axis=0)  7.19 us
  transfers between devices with their start and end apart: 24, of which 12 were waited for; matrix products, arithmetic and copies ran while one was open for 6% of the time, Pallas kernels for 0%

profile of v1, /device:TPU:2, one launch (start us, length us, event | category | flops | bytes accessed | tf_op | source)
XLA Modules:
  0.0 243.6 jit_solution(8188343621935124900)
XLA Ops:
  7.5 3.3 %fusion.76 = f32[16,1,320]{2,1,0:T(1,128)S(1)} fusion(bf16[16,320,320]{2,1,0:T(8,128)(2,1)} %param.27, bf16[16,320,1]{1,0,2:T(8,128)(2,1)S(1)} %convert_bitcast_fusion), kind=kOutput, calls=%fused_computation.136 | convolution fusion | flops 3276800 | bytes 3307520 | tf_op jit(solution)/shard_map/nij,nj->ni/dot_general | solution.py:98
  11.3 7.8 %collective-permute-start.1 = (bf16[16,6,80]{2,1,0:T(8,128)(2,1)S(1)}, bf16[16,6,80]{2,1,0:T(8,128)(2,1)S(1)}, u32[]{:S(2)}, u32[]{:S(2)}) collective-permute-start(bf16[16,6,80]{2,1,0:T(8,128)(2,1)S(1)} %reshape.338), channel_id=1, source_target_pairs={{1,0},{2,1},{3,2},{4,3},{5,4},{6,5},{7,6},{8,7},{9,8},{10,9},{11,1... | collective-permute-start | bytes 46088 | tf_op jit(solution)/shard_map/ppermute | solution.py:16
  21.7 11.4 %all-to-all-start = ((s32[4,2,12]{2,1,0:T(2,128)}), s32[4,2,12]{2,1,0:T(2,128)S(1)}, u32[]{:S(2)}, u32[]{:S(2)}) async-start(s32[4,2,12]{2,1,0:T(2,128)} %stack.2), calls=%async_computation | async-start | bytes 8192 | tf_op jit(solution)/shard_map/all_to_all | solution.py:125
  33.9 3.1 %all-to-all-done = s32[4,2,12]{2,1,0:T(2,128)S(1)} async-done(((s32[4,2,12]{2,1,0:T(2,128)}), s32[4,2,12]{2,1,0:T(2,128)S(1)}, u32[]{:S(2)}, u32[]{:S(2)}) %all-to-all-start) | async-done | bytes 416 | tf_op jit(solution)/shard_map/all_to_all | solution.py:125
  39.0 3.5 %fusion.73 = f32[16,1,320]{2,1,0:T(1,128)S(1)} fusion(bf16[16,320,320]{2,1,0:T(8,128)(2,1)} %param.27, bf16[16,320,1]{1,0,2:T(8,128)(2,1)S(1)} %fusion.18), kind=kOutput, calls=%fused_computation.133 | convolution fusion | flops 3276800 | bytes 3307520 | tf_op jit(solution)/shard_map/nij,nj->ni/dot_general | solution.py:98
  43.0 3.4 %collective-permute-start.3 = (bf16[16,6,80]{2,1,0:T(8,128)(2,1)S(1)}, bf16[16,6,80]{2,1,0:T(8,128)(2,1)S(1)}, u32[]{:S(2)}, u32[]{:S(2)}) collective-permute-start(bf16[16,6,80]{2,1,0:T(8,128)(2,1)S(1)} %reshape.342), channel_id=1, source_target_pairs={{1,0},{2,1},{3,2},{4,3},{5,4},{6,5},{7,6},{8,7},{9,8},{10,9},{11,1... | collective-permute-start | bytes 46088 | tf_op jit(solution)/shard_map/ppermute | solution.py:16
  46.3 2.5 %collective-permute-start.2 = (bf16[16,6,80]{2,1,0:T(8,128)(2,1)S(1)}, bf16[16,6,80]{2,1,0:T(8,128)(2,1)S(1)}, u32[]{:S(2)}, u32[]{:S(2)}) collective-permute-start(bf16[16,6,80]{2,1,0:T(8,128)(2,1)S(1)} %reshape.342), channel_id=1, source_target_pairs={{511,0},{0,1},{1,2},{2,3},{3,4},{4,5},{5,6},{6,7},{7,8},{8,9},{9,1... | collective-permute-start | bytes 46088 | tf_op jit(solution)/shard_map/ppermute | solution.py:16
  49.4 6.1 %collective-permute-done.2 = bf16[16,6,80]{2,1,0:T(8,128)(2,1)S(1)} collective-permute-done((bf16[16,6,80]{2,1,0:T(8,128)(2,1)S(1)}, bf16[16,6,80]{2,1,0:T(8,128)(2,1)S(1)}, u32[]{:S(2)}, u32[]{:S(2)}) %collective-permute-start.2) | collective-permute-done | bytes 15392 | tf_op jit(solution)/shard_map/ppermute | solution.py:16
  57.2 3.3 %fusion.70 = f32[16,1,320]{2,1,0:T(1,128)S(1)} fusion(bf16[16,320,320]{2,1,0:T(8,128)(2,1)} %param.27, bf16[16,320,1]{1,0,2:T(8,128)(2,1)S(1)} %bitcast.136), kind=kOutput, calls=%fused_computation.130 | convolution fusion | flops 3276800 | bytes 3307520 | tf_op jit(solution)/shard_map/nij,nj->ni/dot_general | solution.py:98
  61.0 8.2 %collective-permute-start.5 = (bf16[16,6,80]{2,1,0:T(8,128)(2,1)S(1)}, bf16[16,6,80]{2,1,0:T(8,128)(2,1)S(1)}, u32[]{:S(2)}, u32[]{:S(2)}) collective-permute-start(bf16[16,6,80]{2,1,0:T(8,128)(2,1)S(1)} %reshape.346), channel_id=1, source_target_pairs={{1,0},{2,1},{3,2},{4,3},{5,4},{6,5},{7,6},{8,7},{9,8},{10,9},{11,1... | collective-permute-start | bytes 46088 | tf_op jit(solution)/shard_map/ppermute | solution.py:16
  71.1 3.9 %collective-permute-done.4 = bf16[16,6,80]{2,1,0:T(8,128)(2,1)S(1)} collective-permute-done((bf16[16,6,80]{2,1,0:T(8,128)(2,1)S(1)}, bf16[16,6,80]{2,1,0:T(8,128)(2,1)S(1)}, u32[]{:S(2)}, u32[]{:S(2)}) %collective-permute-start.4) | collective-permute-done | bytes 15392 | tf_op jit(solution)/shard_map/ppermute | solution.py:16
  77.0 17.8 %psum.14 = f32[8,320]{1,0:T(8,128)S(1)} all-reduce(f32[8,320]{1,0:T(8,128)S(1)} %fusion.145), channel_id=1, replica_groups=mesh['fine'=128,'tele'=4] {'tele'}, use_global_device_ids=true, to_apply=%region_3.5 | all-reduce | flops 2560 | bytes 20480 | tf_op jit(solution)/shard_map/psum | solution.py:160
  99.4 2.4 collective-permute-start.6
  101.9 5.9 %collective-permute-done.6 = bf16[8,6,80]{2,1,0:T(8,128)(2,1)S(1)} collective-permute-done((bf16[8,6,80]{2,1,0:T(8,128)(2,1)S(1)}, bf16[8,6,80]{2,1,0:T(8,128)(2,1)S(1)}, u32[]{:S(2)}, u32[]{:S(2)}) %collective-permute-start.6) | collective-permute-done | bytes 7712 | tf_op jit(solution)/shard_map/ppermute | solution.py:16
  114.0 2.4 collective-permute-start.8
  116.4 5.9 %collective-permute-done.8 = bf16[8,6,80]{2,1,0:T(8,128)(2,1)S(1)} collective-permute-done((bf16[8,6,80]{2,1,0:T(8,128)(2,1)S(1)}, bf16[8,6,80]{2,1,0:T(8,128)(2,1)S(1)}, u32[]{:S(2)}, u32[]{:S(2)}) %collective-permute-start.8) | collective-permute-done | bytes 7712 | tf_op jit(solution)/shard_map/ppermute | solution.py:16
  125.7 3.3 %collective-permute-start.11 = (bf16[16,6,80]{2,1,0:T(8,128)(2,1)S(1)}, bf16[16,6,80]{2,1,0:T(8,128)(2,1)S(1)}, u32[]{:S(2)}, u32[]{:S(2)}) collective-permute-start(bf16[16,6,80]{2,1,0:T(8,128)(2,1)S(1)} %reshape.359), channel_id=1, source_target_pairs={{1,0},{2,1},{3,2},{4,3},{5,4},{6,5},{7,6},{8,7},{9,8},{10,9},{11,1... | collective-permute-start | bytes 46088 | tf_op jit(solution)/shard_map/ppermute | solution.py:16
  129.0 2.5 %collective-permute-start.10 = (bf16[16,6,80]{2,1,0:T(8,128)(2,1)S(1)}, bf16[16,6,80]{2,1,0:T(8,128)(2,1)S(1)}, u32[]{:S(2)}, u32[]{:S(2)}) collective-permute-start(bf16[16,6,80]{2,1,0:T(8,128)(2,1)S(1)} %reshape.359), channel_id=1, source_target_pairs={{511,0},{0,1},{1,2},{2,3},{3,4},{4,5},{5,6},{6,7},{7,8},{8,9},{9,1... | collective-permute-start | bytes 46088 | tf_op jit(solution)/shard_map/ppermute | solution.py:16
  131.6 3.3 %collective-permute-done.10 = bf16[16,6,80]{2,1,0:T(8,128)(2,1)S(1)} collective-permute-done((bf16[16,6,80]{2,1,0:T(8,128)(2,1)S(1)}, bf16[16,6,80]{2,1,0:T(8,128)(2,1)S(1)}, u32[]{:S(2)}, u32[]{:S(2)}) %collective-permute-start.10) | collective-permute-done | bytes 15392 | tf_op jit(solution)/shard_map/ppermute | solution.py:16
  136.5 3.3 %fusion.68 = f32[16,1,320]{2,1,0:T(1,128)S(1)} fusion(bf16[16,320,320]{2,1,0:T(8,128)(2,1)} %param.27, bf16[16,320,1]{1,0,2:T(8,128)(2,1)S(1)} %fusion.17), kind=kOutput, calls=%fused_computation.128 | convolution fusion | flops 3276800 | bytes 3307520 | tf_op jit(solution)/shard_map/nij,nj->ni/dot_general | solution.py:98
  140.3 6.9 %collective-permute-start.13 = (bf16[16,6,80]{2,1,0:T(8,128)(2,1)S(1)}, bf16[16,6,80]{2,1,0:T(8,128)(2,1)S(1)}, u32[]{:S(2)}, u32[]{:S(2)}) collective-permute-start(bf16[16,6,80]{2,1,0:T(8,128)(2,1)S(1)} %reshape.363), channel_id=1, source_target_pairs={{1,0},{2,1},{3,2},{4,3},{5,4},{6,5},{7,6},{8,7},{9,8},{10,9},{11,1... | collective-permute-start | bytes 46088 | tf_op jit(solution)/shard_map/ppermute | solution.py:16
  149.3 3.7 %collective-permute-done.12 = bf16[16,6,80]{2,1,0:T(8,128)(2,1)S(1)} collective-permute-done((bf16[16,6,80]{2,1,0:T(8,128)(2,1)S(1)}, bf16[16,6,80]{2,1,0:T(8,128)(2,1)S(1)}, u32[]{:S(2)}, u32[]{:S(2)}) %collective-permute-start.12) | collective-permute-done | bytes 15392 | tf_op jit(solution)/shard_map/ppermute | solution.py:16
  154.7 3.3 %fusion.65 = f32[16,1,320]{2,1,0:T(1,128)S(1)} fusion(bf16[16,320,320]{2,1,0:T(8,128)(2,1)} %param.27, bf16[16,320,1]{1,0,2:T(8,128)(2,1)S(1)} %fusion.16), kind=kOutput, calls=%fused_computation.125 | convolution fusion | flops 3276800 | bytes 3307520 | tf_op jit(solution)/shard_map/nij,nj->ni/dot_general | solution.py:98
  158.4 6.8 %collective-permute-start.15 = (bf16[16,6,80]{2,1,0:T(8,128)(2,1)S(1)}, bf16[16,6,80]{2,1,0:T(8,128)(2,1)S(1)}, u32[]{:S(2)}, u32[]{:S(2)}) collective-permute-start(bf16[16,6,80]{2,1,0:T(8,128)(2,1)S(1)} %reshape.367), channel_id=1, source_target_pairs={{1,0},{2,1},{3,2},{4,3},{5,4},{6,5},{7,6},{8,7},{9,8},{10,9},{11,1... | collective-permute-start | bytes 46088 | tf_op jit(solution)/shard_map/ppermute | solution.py:16
  167.2 3.9 %collective-permute-done.14 = bf16[16,6,80]{2,1,0:T(8,128)(2,1)S(1)} collective-permute-done((bf16[16,6,80]{2,1,0:T(8,128)(2,1)S(1)}, bf16[16,6,80]{2,1,0:T(8,128)(2,1)S(1)}, u32[]{:S(2)}, u32[]{:S(2)}) %collective-permute-start.14) | collective-permute-done | bytes 15392 | tf_op jit(solution)/shard_map/ppermute | solution.py:16
  172.7 3.3 %fusion.62 = f32[16,1,320]{2,1,0:T(1,128)S(1)} fusion(bf16[16,320,320]{2,1,0:T(8,128)(2,1)} %param.27, bf16[16,320,1]{1,0,2:T(8,128)(2,1)S(1)} %bitcast.135), kind=kOutput, calls=%fused_computation.122 | convolution fusion | flops 3276800 | bytes 3307520 | tf_op jit(solution)/shard_map/nij,nj->ni/dot_general | solution.py:98
  176.5 6.8 %collective-permute-start.17 = (bf16[16,6,80]{2,1,0:T(8,128)(2,1)S(1)}, bf16[16,6,80]{2,1,0:T(8,128)(2,1)S(1)}, u32[]{:S(2)}, u32[]{:S(2)}) collective-permute-start(bf16[16,6,80]{2,1,0:T(8,128)(2,1)S(1)} %reshape.371), channel_id=1, source_target_pairs={{1,0},{2,1},{3,2},{4,3},{5,4},{6,5},{7,6},{8,7},{9,8},{10,9},{11,1... | collective-permute-start | bytes 46088 | tf_op jit(solution)/shard_map/ppermute | solution.py:16
  185.2 3.9 %collective-permute-done.16 = bf16[16,6,80]{2,1,0:T(8,128)(2,1)S(1)} collective-permute-done((bf16[16,6,80]{2,1,0:T(8,128)(2,1)S(1)}, bf16[16,6,80]{2,1,0:T(8,128)(2,1)S(1)}, u32[]{:S(2)}, u32[]{:S(2)}) %collective-permute-start.16) | collective-permute-done | bytes 15392 | tf_op jit(solution)/shard_map/ppermute | solution.py:16
  191.1 17.7 %psum.15 = f32[8,320]{1,0:T(8,128)S(1)} all-reduce(f32[8,320]{1,0:T(8,128)S(1)} %fusion.144), channel_id=1, replica_groups=mesh['fine'=128,'tele'=4] {'tele'}, use_global_device_ids=true, to_apply=%region_10.14 | all-reduce | flops 2560 | bytes 20480 | tf_op jit(solution)/shard_map/psum | solution.py:160
  214.2 6.0 %collective-permute-done.18 = bf16[8,6,80]{2,1,0:T(8,128)(2,1)S(1)} collective-permute-done((bf16[8,6,80]{2,1,0:T(8,128)(2,1)S(1)}, bf16[8,6,80]{2,1,0:T(8,128)(2,1)S(1)}, u32[]{:S(2)}, u32[]{:S(2)}) %collective-permute-start.18) | collective-permute-done | bytes 7712 | tf_op jit(solution)/shard_map/ppermute | solution.py:16
  224.8 2.4 collective-permute-start.20
  227.2 6.0 %collective-permute-done.20 = bf16[8,6,80]{2,1,0:T(8,128)(2,1)S(1)} collective-permute-done((bf16[8,6,80]{2,1,0:T(8,128)(2,1)S(1)}, bf16[8,6,80]{2,1,0:T(8,128)(2,1)S(1)}, u32[]{:S(2)}, u32[]{:S(2)}) %collective-permute-start.20) | collective-permute-done | bytes 7712 | tf_op jit(solution)/shard_map/ppermute | solution.py:16
  (181 shorter events, 55.6 us)
Async XLA Ops:
  6.5 31.5 %copy-start = (bf16[24,80,80]{2,1,0:T(8,128)(2,1)S(1)}, bf16[24,80,80]{2,1,0:T(8,128)(2,1)}, u32[]{:S(2)}) copy-start(bf16[24,80,80]{2,1,0:T(8,128)(2,1)} %param.33) | copy-start | bytes 921604
  6.5 26.6 %copy-start.5 = (s32[6]{0:T(128)S(1)}, s32[6]{0:T(128)}, u32[]{:S(2)}) copy-start(s32[6]{0:T(128)} %constant.277.clone) | copy-start | bytes 76
  6.5 32.1 %copy-start.2 = (f32[16,320]{1,0:T(8,128)S(1)}, f32[16,320]{1,0:T(8,128)}, u32[]{:S(2)}) copy-start(f32[16,320]{1,0:T(8,128)} %param.26) | copy-start | bytes 61444
  6.5 14.5 %copy-start.7 = (s32[2,6]{1,0:T(2,128)S(1)}, s32[2,6]{1,0:T(2,128)}, u32[]{:S(2)}) copy-start(s32[2,6]{1,0:T(2,128)} %param.31) | copy-start | bytes 148
  6.5 26.6 %copy-start.3 = (s32[16,6]{0,1:T(8,128)S(1)}, s32[16,6]{0,1:T(8,128)}, u32[]{:S(2)}) copy-start(s32[16,6]{0,1:T(8,128)} %param.28) | copy-start | bytes 1156
  6.6 26.9 %copy-start.8 = (s32[16]{0:T(128)S(1)}, s32[16]{0:T(128)}, u32[]{:S(2)}) copy-start(s32[16]{0:T(128)} %param.34) | copy-start | bytes 196
  6.6 26.9 %copy-start.4 = (s32[16,6]{0,1:T(8,128)S(1)}, s32[16,6]{0,1:T(8,128)}, u32[]{:S(2)}) copy-start(s32[16,6]{0,1:T(8,128)} %param.29) | copy-start | bytes 1156
  6.6 88.1 %all-gather.2.cloned.1.call-start = ((), (), s32[]{:S(2)}) async-start(), calls=%async_computation.1 | async-start | bytes 2457600 | tf_op jit(solution)/shard_map/all_gather | solution.py:123
  11.3 26.0 %collective-permute-start.1 = (bf16[16,6,80]{2,1,0:T(8,128)(2,1)S(1)}, bf16[16,6,80]{2,1,0:T(8,128)(2,1)S(1)}, u32[]{:S(2)}, u32[]{:S(2)}) collective-permute-start(bf16[16,6,80]{2,1,0:T(8,128)(2,1)S(1)} %reshape.338), channel_id=1, source_target_pairs={{1,0},{2,1},{3,2},{4,3},{5,4},{6,5},{7,6},{8,7},{9,8},{10,9},{11,1... | collective-permute-start | bytes 46088 | tf_op jit(solution)/shard_map/ppermute | solution.py:16
  19.1 18.2 %collective-permute-start = (bf16[16,6,80]{2,1,0:T(8,128)(2,1)S(1)}, bf16[16,6,80]{2,1,0:T(8,128)(2,1)S(1)}, u32[]{:S(2)}, u32[]{:S(2)}) collective-permute-start(bf16[16,6,80]{2,1,0:T(8,128)(2,1)S(1)} %reshape.338), channel_id=1, source_target_pairs={{511,0},{0,1},{1,2},{2,3},{3,4},{4,5},{5,6},{6,7},{7,8},{8,9},{9,1... | collective-permute-start | bytes 46088 | tf_op jit(solution)/shard_map/ppermute | solution.py:16
  21.7 15.3 %all-to-all-start = ((s32[4,2,12]{2,1,0:T(2,128)}), s32[4,2,12]{2,1,0:T(2,128)S(1)}, u32[]{:S(2)}, u32[]{:S(2)}) async-start(s32[4,2,12]{2,1,0:T(2,128)} %stack.2), calls=%async_computation | async-start | bytes 8192 | tf_op jit(solution)/shard_map/all_to_all | solution.py:125
  43.0 6.5 %collective-permute-start.3 = (bf16[16,6,80]{2,1,0:T(8,128)(2,1)S(1)}, bf16[16,6,80]{2,1,0:T(8,128)(2,1)S(1)}, u32[]{:S(2)}, u32[]{:S(2)}) collective-permute-start(bf16[16,6,80]{2,1,0:T(8,128)(2,1)S(1)} %reshape.342), channel_id=1, source_target_pairs={{1,0},{2,1},{3,2},{4,3},{5,4},{6,5},{7,6},{8,7},{9,8},{10,9},{11,1... | collective-permute-start | bytes 46088 | tf_op jit(solution)/shard_map/ppermute | solution.py:16
  46.3 9.2 %collective-permute-start.2 = (bf16[16,6,80]{2,1,0:T(8,128)(2,1)S(1)}, bf16[16,6,80]{2,1,0:T(8,128)(2,1)S(1)}, u32[]{:S(2)}, u32[]{:S(2)}) collective-permute-start(bf16[16,6,80]{2,1,0:T(8,128)(2,1)S(1)} %reshape.342), channel_id=1, source_target_pairs={{511,0},{0,1},{1,2},{2,3},{3,4},{4,5},{5,6},{6,7},{7,8},{8,9},{9,1... | collective-permute-start | bytes 46088 | tf_op jit(solution)/shard_map/ppermute | solution.py:16
  61.0 10.2 %collective-permute-start.5 = (bf16[16,6,80]{2,1,0:T(8,128)(2,1)S(1)}, bf16[16,6,80]{2,1,0:T(8,128)(2,1)S(1)}, u32[]{:S(2)}, u32[]{:S(2)}) collective-permute-start(bf16[16,6,80]{2,1,0:T(8,128)(2,1)S(1)} %reshape.346), channel_id=1, source_target_pairs={{1,0},{2,1},{3,2},{4,3},{5,4},{6,5},{7,6},{8,7},{9,8},{10,9},{11,1... | collective-permute-start | bytes 46088 | tf_op jit(solution)/shard_map/ppermute | solution.py:16
  69.2 5.8 %collective-permute-start.4 = (bf16[16,6,80]{2,1,0:T(8,128)(2,1)S(1)}, bf16[16,6,80]{2,1,0:T(8,128)(2,1)S(1)}, u32[]{:S(2)}, u32[]{:S(2)}) collective-permute-start(bf16[16,6,80]{2,1,0:T(8,128)(2,1)S(1)} %reshape.346), channel_id=1, source_target_pairs={{511,0},{0,1},{1,2},{2,3},{3,4},{4,5},{5,6},{6,7},{7,8},{8,9},{9,1... | collective-permute-start | bytes 46088 | tf_op jit(solution)/shard_map/ppermute | solution.py:16
  94.7 29.3 %copy-start.1 = (bf16[8,320,320]{2,1,0:T(8,128)(2,1)S(1)}, bf16[8,320,320]{2,1,0:T(8,128)(2,1)}, u32[]{:S(2)}) copy-start(bf16[8,320,320]{2,1,0:T(8,128)(2,1)} %all-gather.2.cloned.1.call-done) | copy-start | bytes 4915204
  97.5 4.4 %collective-permute-start.7 = (bf16[8,6,80]{2,1,0:T(8,128)(2,1)S(1)}, bf16[8,6,80]{2,1,0:T(8,128)(2,1)S(1)}, u32[]{:S(2)}, u32[]{:S(2)}) collective-permute-start(bf16[8,6,80]{2,1,0:T(8,128)(2,1)S(1)} %reshape.351), channel_id=1, source_target_pairs={{4,0},{8,4},{12,8},{16,12},{20,16},{24,20},{28,24},{32,28},{36,32}... | collective-permute-start | bytes 23048 | tf_op jit(solution)/shard_map/ppermute | solution.py:16
  99.4 8.4 %collective-permute-start.6 = (bf16[8,6,80]{2,1,0:T(8,128)(2,1)S(1)}, bf16[8,6,80]{2,1,0:T(8,128)(2,1)S(1)}, u32[]{:S(2)}, u32[]{:S(2)}) collective-permute-start(bf16[8,6,80]{2,1,0:T(8,128)(2,1)S(1)} %reshape.351), channel_id=1, source_target_pairs={{508,0},{0,4},{4,8},{8,12},{12,16},{16,20},{20,24},{24,28},{28,32}... | collective-permute-start | bytes 23048 | tf_op jit(solution)/shard_map/ppermute | solution.py:16
  112.0 4.4 %collective-permute-start.9 = (bf16[8,6,80]{2,1,0:T(8,128)(2,1)S(1)}, bf16[8,6,80]{2,1,0:T(8,128)(2,1)S(1)}, u32[]{:S(2)}, u32[]{:S(2)}) collective-permute-start(bf16[8,6,80]{2,1,0:T(8,128)(2,1)S(1)} %reshape.355), channel_id=1, source_target_pairs={{4,0},{8,4},{12,8},{16,12},{20,16},{24,20},{28,24},{32,28},{36,32}... | collective-permute-start | bytes 23048 | tf_op jit(solution)/shard_map/ppermute | solution.py:16
  114.0 8.4 %collective-permute-start.8 = (bf16[8,6,80]{2,1,0:T(8,128)(2,1)S(1)}, bf16[8,6,80]{2,1,0:T(8,128)(2,1)S(1)}, u32[]{:S(2)}, u32[]{:S(2)}) collective-permute-start(bf16[8,6,80]{2,1,0:T(8,128)(2,1)S(1)} %reshape.355), channel_id=1, source_target_pairs={{508,0},{0,4},{4,8},{8,12},{12,16},{16,20},{20,24},{24,28},{28,32}... | collective-permute-start | bytes 23048 | tf_op jit(solution)/shard_map/ppermute | solution.py:16
  125.7 5.9 %collective-permute-start.11 = (bf16[16,6,80]{2,1,0:T(8,128)(2,1)S(1)}, bf16[16,6,80]{2,1,0:T(8,128)(2,1)S(1)}, u32[]{:S(2)}, u32[]{:S(2)}) collective-permute-start(bf16[16,6,80]{2,1,0:T(8,128)(2,1)S(1)} %reshape.359), channel_id=1, source_target_pairs={{1,0},{2,1},{3,2},{4,3},{5,4},{6,5},{7,6},{8,7},{9,8},{10,9},{11,1... | collective-permute-start | bytes 46088 | tf_op jit(solution)/shard_map/ppermute | solution.py:16
  129.0 5.8 %collective-permute-start.10 = (bf16[16,6,80]{2,1,0:T(8,128)(2,1)S(1)}, bf16[16,6,80]{2,1,0:T(8,128)(2,1)S(1)}, u32[]{:S(2)}, u32[]{:S(2)}) collective-permute-start(bf16[16,6,80]{2,1,0:T(8,128)(2,1)S(1)} %reshape.359), channel_id=1, source_target_pairs={{511,0},{0,1},{1,2},{2,3},{3,4},{4,5},{5,6},{6,7},{7,8},{8,9},{9,1... | collective-permute-start | bytes 46088 | tf_op jit(solution)/shard_map/ppermute | solution.py:16
  140.3 9.0 %collective-permute-start.13 = (bf16[16,6,80]{2,1,0:T(8,128)(2,1)S(1)}, bf16[16,6,80]{2,1,0:T(8,128)(2,1)S(1)}, u32[]{:S(2)}, u32[]{:S(2)}) collective-permute-start(bf16[16,6,80]{2,1,0:T(8,128)(2,1)S(1)} %reshape.363), channel_id=1, source_target_pairs={{1,0},{2,1},{3,2},{4,3},{5,4},{6,5},{7,6},{8,7},{9,8},{10,9},{11,1... | collective-permute-start | bytes 46088 | tf_op jit(solution)/shard_map/ppermute | solution.py:16
  147.2 5.8 %collective-permute-start.12 = (bf16[16,6,80]{2,1,0:T(8,128)(2,1)S(1)}, bf16[16,6,80]{2,1,0:T(8,128)(2,1)S(1)}, u32[]{:S(2)}, u32[]{:S(2)}) collective-permute-start(bf16[16,6,80]{2,1,0:T(8,128)(2,1)S(1)} %reshape.363), channel_id=1, source_target_pairs={{511,0},{0,1},{1,2},{2,3},{3,4},{4,5},{5,6},{6,7},{7,8},{8,9},{9,1... | collective-permute-start | bytes 46088 | tf_op jit(solution)/shard_map/ppermute | solution.py:16
  158.4 8.7 %collective-permute-start.15 = (bf16[16,6,80]{2,1,0:T(8,128)(2,1)S(1)}, bf16[16,6,80]{2,1,0:T(8,128)(2,1)S(1)}, u32[]{:S(2)}, u32[]{:S(2)}) collective-permute-start(bf16[16,6,80]{2,1,0:T(8,128)(2,1)S(1)} %reshape.367), channel_id=1, source_target_pairs={{1,0},{2,1},{3,2},{4,3},{5,4},{6,5},{7,6},{8,7},{9,8},{10,9},{11,1... | collective-permute-start | bytes 46088 | tf_op jit(solution)/shard_map/ppermute | solution.py:16
  165.2 5.8 %collective-permute-start.14 = (bf16[16,6,80]{2,1,0:T(8,128)(2,1)S(1)}, bf16[16,6,80]{2,1,0:T(8,128)(2,1)S(1)}, u32[]{:S(2)}, u32[]{:S(2)}) collective-permute-start(bf16[16,6,80]{2,1,0:T(8,128)(2,1)S(1)} %reshape.367), channel_id=1, source_target_pairs={{511,0},{0,1},{1,2},{2,3},{3,4},{4,5},{5,6},{6,7},{7,8},{8,9},{9,1... | collective-permute-start | bytes 46088 | tf_op jit(solution)/shard_map/ppermute | solution.py:16
  176.5 8.7 %collective-permute-start.17 = (bf16[16,6,80]{2,1,0:T(8,128)(2,1)S(1)}, bf16[16,6,80]{2,1,0:T(8,128)(2,1)S(1)}, u32[]{:S(2)}, u32[]{:S(2)}) collective-permute-start(bf16[16,6,80]{2,1,0:T(8,128)(2,1)S(1)} %reshape.371), channel_id=1, source_target_pairs={{1,0},{2,1},{3,2},{4,3},{5,4},{6,5},{7,6},{8,7},{9,8},{10,9},{11,1... | collective-permute-start | bytes 46088 | tf_op jit(solution)/shard_map/ppermute | solution.py:16
  183.3 5.9 %collective-permute-start.16 = (bf16[16,6,80]{2,1,0:T(8,128)(2,1)S(1)}, bf16[16,6,80]{2,1,0:T(8,128)(2,1)S(1)}, u32[]{:S(2)}, u32[]{:S(2)}) collective-permute-start(bf16[16,6,80]{2,1,0:T(8,128)(2,1)S(1)} %reshape.371), channel_id=1, source_target_pairs={{511,0},{0,1},{1,2},{2,3},{3,4},{4,5},{5,6},{6,7},{7,8},{8,9},{9,1... | collective-permute-start | bytes 46088 | tf_op jit(solution)/shard_map/ppermute | solution.py:16
  209.8 4.3 %collective-permute-start.19 = (bf16[8,6,80]{2,1,0:T(8,128)(2,1)S(1)}, bf16[8,6,80]{2,1,0:T(8,128)(2,1)S(1)}, u32[]{:S(2)}, u32[]{:S(2)}) collective-permute-start(bf16[8,6,80]{2,1,0:T(8,128)(2,1)S(1)} %reshape.375), channel_id=1, source_target_pairs={{4,0},{8,4},{12,8},{16,12},{20,16},{24,20},{28,24},{32,28},{36,32}... | collective-permute-start | bytes 23048 | tf_op jit(solution)/shard_map/ppermute | solution.py:16
  211.8 8.4 %collective-permute-start.18 = (bf16[8,6,80]{2,1,0:T(8,128)(2,1)S(1)}, bf16[8,6,80]{2,1,0:T(8,128)(2,1)S(1)}, u32[]{:S(2)}, u32[]{:S(2)}) collective-permute-start(bf16[8,6,80]{2,1,0:T(8,128)(2,1)S(1)} %reshape.375), channel_id=1, source_target_pairs={{508,0},{0,4},{4,8},{8,12},{12,16},{16,20},{20,24},{24,28},{28,32}... | collective-permute-start | bytes 23048 | tf_op jit(solution)/shard_map/ppermute | solution.py:16
  222.9 4.3 %collective-permute-start.21 = (bf16[8,6,80]{2,1,0:T(8,128)(2,1)S(1)}, bf16[8,6,80]{2,1,0:T(8,128)(2,1)S(1)}, u32[]{:S(2)}, u32[]{:S(2)}) collective-permute-start(bf16[8,6,80]{2,1,0:T(8,128)(2,1)S(1)} %reshape.379), channel_id=1, source_target_pairs={{4,0},{8,4},{12,8},{16,12},{20,16},{24,20},{28,24},{32,28},{36,32}... | collective-permute-start | bytes 23048 | tf_op jit(solution)/shard_map/ppermute | solution.py:16
  224.8 8.4 %collective-permute-start.20 = (bf16[8,6,80]{2,1,0:T(8,128)(2,1)S(1)}, bf16[8,6,80]{2,1,0:T(8,128)(2,1)S(1)}, u32[]{:S(2)}, u32[]{:S(2)}) collective-permute-start(bf16[8,6,80]{2,1,0:T(8,128)(2,1)S(1)} %reshape.379), channel_id=1, source_target_pairs={{508,0},{0,4},{4,8},{8,12},{12,16},{16,20},{20,24},{24,28},{28,32}... | collective-permute-start | bytes 23048 | tf_op jit(solution)/shard_map/ppermute | solution.py:16
  (1 other events, 14.5 us)
Sparse Core Ops, SparseCore 0:
  21.2 38.3 all-gather.1
